TPU v7x, 256 devices: a whole 4x4x8 slice. The times are simulated.
256 devices in a mesh: ctx: 16 (over x_hi, y, core), exp: 16 (over z, x_lo).
Axes of the slice: x: 4 (x_hi: 2, x_lo: 2; x = x_hi * 2 + x_lo), y: 4, z: 8, core: 2. Of those that a mesh axis runs over, the one named last changes fastest.
Arguments:
- query: bfloat16 [1024, 8192], P('ctx', 'exp'), may hold values from -7 to 7
- keys: bfloat16 [32768, 512], P('ctx'), may hold values from -9 to 9
- values: bfloat16 [32768, 512], P('ctx'), may hold values from -6 to 6
- out_weight: bfloat16 [8192, 4096], P('exp'), may hold values from -3 to 3
- residual: bfloat16 [1024, 4096], P(('ctx', 'exp')), may hold values from -6 to 6
- norm_gain: float32 [4096], replicated, may hold values from 0.1 to 1.9
- expert_ids: int32 [1024, 8], P(('ctx', 'exp')), may hold values from 0 to 31, all different within a row; in each aligned block of 4 rows (0 to 3, 4 to 7, ...) at most 2 rows name the same one
- gate_values: float32 [1024, 8], P(('ctx', 'exp')), may hold values from 0.05 to 1
- w_gate_up: bfloat16 [32, 4096, 3072], P('exp', 'ctx'), may hold values from -0.09375 to 0.09375
- w_down: bfloat16 [32, 1536, 4096], P('exp', None, 'ctx'), may hold values from -0.15625 to 0.15625
Outputs:
- layer_out: float32 [1024, 4096], P(('ctx', 'exp'))
- head_max: float32 [64], P('exp')
Inputs may be any that keep to these rules, and one draw needn't show every extreme that they name: `expert_ids`: each row names 8 different experts; in the rows of one device no expert is named more than 2 times.
All inputs are finite; a program needn't handle non-finite values.
Results may differ from a plain program's by a relative error of at most 0.018.
Values may be sent and summed in bfloat16 or wider, within the bound.
A program may use at most 192 MiB of HBM per device.

v0:
```python
import math
import jax
import jax.numpy as jnp
from jax import lax
from jax.sharding import PartitionSpec as P

D = 4096
HEADS = 64
KVH = 4
HD = 128
FF = 1536
TOP = 8
EXPERTS = 32
eps = 1e-06


def attend_block(carry_state, q_rows, k_block, v_block, q_pos):
    weighted, row_peak, row_total = carry_state
    score_scale = 1.0 / math.sqrt(q_rows.shape[1])
    scores = (
        jnp.einsum("rd,kd->rk", q_rows, k_block, preferred_element_type=jnp.float32) * score_scale
    )
    k_pos = jnp.arange(k_block.shape[0], dtype=jnp.int32)
    visible = k_pos[None, :] <= q_pos[:, None]
    masked = jnp.where(visible, scores, -1e30)
    new_peak = jnp.maximum(row_peak, jnp.max(masked, axis=1))
    weights = jnp.where(visible, jnp.exp(masked - new_peak[:, None]), 0.0)
    row_total = jnp.sum(weights, axis=1)
    weighted = jnp.dot(weights.astype(jnp.bfloat16), v_block, preferred_element_type=jnp.float32)
    return (weighted, new_peak, row_total)


def local(
    query, keys, values, out_weight, residual, norm_gain, expert_ids, gate_values, w_gate_up, w_down
):
    ctx_count = lax.axis_size("ctx")
    exp_count = lax.axis_size("exp")
    ctx_index = lax.axis_index("ctx")
    exp_index = lax.axis_index("exp")
    q_local, q_width = query.shape
    head_count = q_width // HD
    key_local = keys.shape[0]
    length = key_local * ctx_count
    slab_rows = q_local * ctx_count
    kv_index = exp_index * head_count // (HEADS // KVH)
    k_head = lax.dynamic_slice_in_dim(keys, kv_index * HD, HD, 1)
    v_head = lax.dynamic_slice_in_dim(values, kv_index * HD, HD, 1)
    q_rows = (
        query.reshape(q_local, head_count, HD).transpose(1, 0, 2).reshape(head_count * q_local, HD)
    )
    row_offsets = jnp.tile(jnp.arange(q_local, dtype=jnp.int32), head_count)
    flat_rows = head_count * q_local
    start_state = (
        jnp.zeros((flat_rows, HD), jnp.float32),
        jnp.full((flat_rows,), -1e30, jnp.float32),
        jnp.zeros((flat_rows,), jnp.float32),
    )
    q_pos = length - slab_rows + ctx_index * q_local + row_offsets
    weighted, row_peak, row_total = attend_block(
        start_state,
        q_rows,
        lax.all_gather(k_head, "ctx", axis=0, tiled=True),
        lax.all_gather(v_head, "ctx", axis=0, tiled=True),
        q_pos,
    )
    attended = (weighted / row_total[:, None]).astype(jnp.bfloat16)
    attended = (
        attended.reshape(head_count, q_local, HD)
        .transpose(1, 0, 2)
        .reshape(q_local, head_count * HD)
    )
    head_peak = jnp.max(row_peak.reshape(head_count, q_local), axis=1)
    head_max = lax.pmax(head_peak, "ctx")
    part_rows = attended
    projected = lax.psum_scatter(
        jnp.dot(part_rows, out_weight, preferred_element_type=jnp.float32),
        "exp",
        scatter_dimension=0,
        tiled=True,
    )
    state_rows = residual.astype(jnp.float32) + projected
    normed = (
        state_rows
        * lax.rsqrt(jnp.mean(state_rows * state_rows, axis=1, keepdims=True) + eps)
        * norm_gain
    ).astype(jnp.bfloat16)
    local_rows = normed.shape[0]
    slot_cap = max(2, 2 * local_rows * TOP // EXPERTS)
    slot_count = slot_cap * EXPERTS
    flat_ids = expert_ids.reshape(-1)
    onehot_ids = (flat_ids[:, None] == jnp.arange(EXPERTS, dtype=jnp.int32)[None, :]).astype(
        jnp.int32
    )
    earlier = jnp.cumsum(onehot_ids, axis=0) - onehot_ids
    slot_rank = jnp.sum(earlier * onehot_ids, axis=1)
    target = slot_rank * EXPERTS + flat_ids
    slot_table = target[None, :] == jnp.arange(slot_count, dtype=jnp.int32)[:, None]
    place_rows = jnp.any(slot_table.reshape(slot_count, local_rows, TOP), axis=2).astype(
        jnp.bfloat16
    )
    outgoing = jnp.dot(place_rows, normed, preferred_element_type=jnp.float32).astype(jnp.bfloat16)
    outgoing = outgoing.reshape(1, 1, slot_cap, EXPERTS, D)
    incoming = lax.all_to_all(
        lax.all_to_all(outgoing, "ctx", split_axis=4, concat_axis=1, tiled=True),
        "exp",
        split_axis=3,
        concat_axis=0,
        tiled=True,
    )
    expert_local = w_down.shape[0]
    d_local = w_gate_up.shape[1]
    expert_rows = incoming.reshape(-1, expert_local, d_local)
    part_rows = expert_rows
    summed = lax.psum(
        jnp.einsum("mxd,xdf->mxf", part_rows, w_gate_up, preferred_element_type=jnp.float32).astype(
            jnp.bfloat16
        ),
        "ctx",
    ).astype(jnp.float32)
    inner_units = (jax.nn.silu(summed[..., :FF]) * summed[..., FF:]).astype(jnp.bfloat16)
    expert_out = jnp.einsum(
        "mxf,xfd->mxd", inner_units, w_down, preferred_element_type=jnp.float32
    ).astype(jnp.bfloat16)
    shaped = expert_out.reshape(exp_count, ctx_count, slot_cap, expert_local, d_local)
    returned = lax.all_to_all(
        lax.all_to_all(shaped, "ctx", split_axis=1, concat_axis=4, tiled=True),
        "exp",
        split_axis=0,
        concat_axis=3,
        tiled=True,
    )
    back_rows = returned.reshape(slot_count, D)
    pick_table = (target[:, None] == jnp.arange(slot_count, dtype=jnp.int32)[None, :]).astype(
        jnp.bfloat16
    )
    per_choice = jnp.dot(pick_table, back_rows, preferred_element_type=jnp.float32).reshape(
        local_rows, TOP, D
    )
    moe_sum = jnp.sum(per_choice * gate_values[:, :, None], axis=1)
    layer_out = state_rows + moe_sum
    return (layer_out, head_max)


def solution(mesh):
    return jax.shard_map(
        local,
        mesh=mesh,
        in_specs=(
            P("ctx", "exp"),
            P("ctx", None),
            P("ctx", None),
            P("exp", None),
            P(("ctx", "exp"), None),
            P(),
            P(("ctx", "exp"), None),
            P(("ctx", "exp"), None),
            P("exp", "ctx", None),
            P("exp", None, "ctx"),
        ),
        out_specs=(P(("ctx", "exp"), None), P("exp")),
        check_vma=False,
    )
```

profile of v0, /device:TPU:6, one launch (start us, length us, event | category | flops | bytes accessed | tf_op | source)
XLA Modules:
  0.0 649.4 jit_solution(4348917887009457203)
XLA Ops:
  12.3 77.6 %all-gather.3.cloned.1.call-done = bf16[32768,128]{1,0:T(8,128)(2,1)} async-done(((bf16[2048,128]{1,0:T(8,128)(2,1)}), bf16[32768,128]{1,0:T(8,128)(2,1)}) %all-gather.3.cloned.1.call-update) | async-done | bytes 8388624 | tf_op jit(solution)/shard_map/all_gather | solution.py:62
  89.8 19.2 %fusion.36 = (f32[256]{0:T(256)S(1)}, f32[256,32768]{0,1:T(8,128)}) fusion(bf16[32768,128]{1,0:T(8,128)(2,1)} %all-gather.3.cloned.1.call-done, bf16[256,128]{1,0:T(8,128)(2,1)S(1)} %bitcast.61, s32[256]{0:T(256)S(1)} %add.53), kind=kOutput, calls=%fused_computation.45 | convolution fusion | flops 2181037824 | bytes 42010624 | tf_op jit(solution)/shard_map/rd,kd->rk/dot_general | solution.py:21
  109.1 15.1 %fusion.2 = f32[256]{0:T(256)S(1)} fusion(f32[256,32768]{0,1:T(8,128)} %get-tuple-element.3, f32[256]{0:T(256)S(1)} %broadcast_maximum_fusion, s32[256]{0:T(256)S(1)} %add.53), kind=kLoop, calls=%fused_computation.5 | loop fusion | flops 33554176 | bytes 33557504 | tf_op jit(solution)/shard_map/reduce_sum | solution.py:28
  124.3 43.9 %all-gather.5.cloned.1.call-done = bf16[32768,128]{1,0:T(8,128)(2,1)} async-done(((bf16[2048,128]{1,0:T(8,128)(2,1)}), bf16[32768,128]{1,0:T(8,128)(2,1)}) %all-gather.5.cloned.1.call-update) | async-done | bytes 8388624 | tf_op jit(solution)/shard_map/all_gather | solution.py:63
  168.2 17.2 %fusion.19 = bf16[256,128]{1,0:T(8,128)(2,1)S(1)} fusion(bf16[32768,128]{1,0:T(8,128)(2,1)} %all-gather.5.cloned.1.call-done, f32[256,32768]{0,1:T(8,128)} %get-tuple-element.3, f32[256]{0:T(256)S(1)} %broadcast_maximum_fusion, s32[256]{0:T(256)S(1)} %add.53, f32[256]{0:T(256)S(1)} %fusion.2), kind=kOutput, calls=%fused_computation.18 | convolution fusion | flops 2181103616 | bytes 42011648 | tf_op jit(solution)/shard_map/dot_general | solution.py:29
  185.4 4.0 fusion.22
  191.6 137.2 %all-reduce.6.cloned.1.call-done = f32[64,4096]{1,0:T(8,128)} async-done(((f32[64,4096]{1,0:T(8,128)}), f32[64,4096]{1,0:T(8,128)}) %all-reduce.6.cloned.1.call-update) | async-done | bytes 1048592
  329.8 2.1 convolution_convert_fusion
  331.9 5.3 copy.33
  337.2 5.9 reshape.120
  343.1 16.8 %all_to_all.66 = bf16[16,2,8192]{2,1,0:T(2,128)(2,1)} all-to-all(bf16[16,2,8192]{2,1,0:T(2,128)(2,1)} %reshape.120), channel_id=1, replica_groups=mesh['ctx'=16,'exp'=16] {'ctx'}, dimensions={0} | all-to-all | bytes 1048576 | tf_op jit(solution)/shard_map/all_to_all | solution.py:104
  359.8 5.9 reshape.121
  365.7 4.1 copy.34
  369.9 23.2 %all_to_all.67 = bf16[1,16,2,32,256]{4,1,2,0,3:T(8,128)(2,1)S(1)} all-to-all(bf16[1,16,2,32,256]{4,1,2,0,3:T(8,128)(2,1)} %bitcast.56), channel_id=1, replica_groups=mesh['ctx'=16,'exp'=16] {'exp'}, dimensions={3} | all-to-all | bytes 1048576 | tf_op jit(solution)/shard_map/all_to_all | solution.py:103
  394.5 2.0 reshape.113
  396.5 5.5 convert_bitcast_fusion
  402.1 157.1 %all-reduce.4.cloned.1.call-done = bf16[512,2,3072]{2,0,1:T(8,128)(2,1)} async-done(((bf16[512,2,3072]{2,0,1:T(8,128)(2,1)}), bf16[512,2,3072]{2,0,1:T(8,128)(2,1)}) %all-reduce.4.cloned.1.call-update) | async-done | bytes 6291472 | tf_op jit(solution)/shard_map/psum | solution.py:114
  559.2 4.5 convert_element_type.46
  563.7 2.7 fusion.12
  566.4 2.1 reshape.114
  569.8 16.8 %all_to_all.68 = bf16[16,16,2,2,256]{4,0,3,2,1:T(8,128)(2,1)S(1)} all-to-all(bf16[16,16,2,2,256]{4,0,3,2,1:T(8,128)(2,1)S(1)} %copy.37), channel_id=1, replica_groups=mesh['ctx'=16,'exp'=16] {'ctx'}, dimensions={1} | all-to-all | bytes 1048576 | tf_op jit(solution)/shard_map/all_to_all | solution.py:126
  589.7 8.5 %all-to-all-start.3 = ((bf16[16,1,2,2,4096]{4,3,2,1,0:T(2,128)(2,1)}), bf16[16,1,2,2,4096]{4,3,2,1,0:T(2,128)(2,1)}, u32[]{:S(2)}, u32[]{:S(2)}) async-start(bf16[16,1,2,2,4096]{4,3,2,1,0:T(2,128)(2,1)} %reshape.117), calls=%async_computation.3 | async-start | bytes 1048576 | tf_op jit(solution)/shard_map/all_to_all | solution.py:125
  598.4 37.2 %pmax.7 = f32[4]{0:T(128)} all-reduce(f32[4]{0:T(128)S(1)} %reduce_max.19), channel_id=1, replica_groups=mesh['ctx'=16,'exp'=16] {'ctx'}, use_global_device_ids=true, to_apply=%region_10.11 | all-reduce | flops 4 | bytes 32 | tf_op jit(solution)/shard_map/pmax | solution.py:73
  635.6 2.3 copy.40
  (52 shorter events, 18.6 us)
Async XLA Ops:
  7.2 389.4 %copy-start = (bf16[2,256,3072]{2,1,0:T(8,128)(2,1)S(1)}, bf16[2,256,3072]{2,1,0:T(8,128)(2,1)}, u32[]{:S(2)}) copy-start(bf16[2,256,3072]{2,1,0:T(8,128)(2,1)} %param.18) | copy-start | bytes 9437188
  7.2 82.7 %all-gather.3.cloned.1.call-start = ((), (), s32[]{:S(2)}) async-start(), calls=%async_computation.4 | async-start | bytes 8912896 | tf_op jit(solution)/shard_map/all_gather | solution.py:62
  9.3 158.9 %all-gather.5.cloned.1.call-start = ((), (), s32[]{:S(2)}) async-start(), calls=%async_computation.5 | async-start | bytes 8912896 | tf_op jit(solution)/shard_map/all_gather | solution.py:63
  11.2 317.5 %all-reduce.6.cloned.1.call-start = ((), (), s32[]{:S(2)}) async-start(), calls=%async_computation.7 | async-start | bytes 2097152
  124.2 65.5 %copy-start.3 = (s32[4,8]{1,0:T(4,128)S(1)}, s32[4,8]{1,0:T(4,128)}, u32[]{:S(2)}) copy-start(s32[4,8]{1,0:T(4,128)} %param.16) | copy-start | bytes 388
  124.2 66.0 %copy-start.6 = (u32[256]{0:T(256)S(1)}, u32[256]{0:T(256)}, u32[]{:S(2)}) copy-start(u32[256]{0:T(256)} %constant.65) | copy-start | bytes 3076
  124.2 204.5 %copy-start.1 = (bf16[4,4096]{1,0:T(4,128)(2,1)S(1)}, bf16[4,4096]{1,0:T(4,128)(2,1)}, u32[]{:S(2)}) copy-start(bf16[4,4096]{1,0:T(4,128)(2,1)} %param.14) | copy-start | bytes 98308
  124.2 205.6 %copy-start.2 = (f32[4096]{0:T(1024)S(1)}, f32[4096]{0:T(1024)}, u32[]{:S(2)}) copy-start(f32[4096]{0:T(1024)} %param.15) | copy-start | bytes 49156
  189.5 369.7 %all-reduce.4.cloned.1.call-start = ((), (), s32[]{:S(2)}) async-start(), calls=%async_computation.6 | async-start | bytes 12582912 | tf_op jit(solution)/shard_map/psum | solution.py:114
  559.2 4.6 copy-start.5
  566.4 73.5 %copy-start.4 = (f32[4,8]{1,0:T(4,128)S(1)}, f32[4,8]{1,0:T(4,128)}, u32[]{:S(2)}) copy-start(f32[4,8]{1,0:T(4,128)} %param.17) | copy-start | bytes 388
  589.7 45.9 %all-to-all-start.3 = ((bf16[16,1,2,2,4096]{4,3,2,1,0:T(2,128)(2,1)}), bf16[16,1,2,2,4096]{4,3,2,1,0:T(2,128)(2,1)}, u32[]{:S(2)}, u32[]{:S(2)}) async-start(bf16[16,1,2,2,4096]{4,3,2,1,0:T(2,128)(2,1)} %reshape.117), calls=%async_computation.3 | async-start | bytes 1048576 | tf_op jit(solution)/shard_map/all_to_all | solution.py:125
Sparse Core Ops, SparseCore 0:
  10.7 79.0 all-gather.2
  92.6 75.5 all-gather.4
  189.6 139.0 all-reduce.5
  402.2 156.9 all-reduce.3
where the time goes:
time: 651 us; the launch traced here: 649 us
  waiting for transfers between devices  416 us (64%)
  blocking collectives  94 us (14%)
  matrix products  52.1 us (8%)
  local copies, waits for them, and re-layouts  41.2 us (6%)
  other arithmetic  22.8 us (4%)
  between operations  14.6 us (2%)
  starting transfers between devices  8.83 us (1%)
    psum x1, waiting for transfers between devices, local(): lax.psum(jnp.einsum('mxd,xdf->mxf', part_rows, w_gate_up, preferred_eleme...  157 us
    unnamed x5, waiting for transfers between devices  137 us
    all_gather x1, waiting for transfers between devices, local(): lax.all_gather(k_head, 'ctx', axis=0, tiled=True)  77.6 us
    all_gather x1, waiting for transfers between devices, local(): lax.all_gather(v_head, 'ctx', axis=0, tiled=True)  43.9 us
    pmax x1, blocking collectives, local(): head_max = lax.pmax(head_peak, 'ctx')  37.2 us
    all_to_all x1, blocking collectives, local(): lax.all_to_all(lax.all_to_all(outgoing, 'ctx', split_axis=4, concat_axis=...  23.2 us
    dot_general x1, matrix products, attend_block(): jnp.einsum('rd,kd->rk', q_rows, k_block, preferred_element_type=jnp.float32)  19.2 us
    dot_general x1, matrix products, attend_block(): jnp.dot(weights.astype(jnp.bfloat16), v_block, preferred_element_type=jnp...  17.2 us
  transfers between devices with their start and end apart: 5, of which 4 were waited for; matrix products, arithmetic and copies ran while one was open for 6% of the time, Pallas kernels for 0%

commit v1 on v0

--- a/solution.py
+++ b/solution.py
@@ -59,7 +59,15 @@
     weighted, row_peak, row_total = attend_block(
         start_state,
         q_rows,
-        lax.all_gather(k_head, "ctx", axis=0, tiled=True),
+        jnp.concatenate(
+            lax.all_to_all(
+                jnp.stack([k_head for _ in range(lax.axis_size("ctx"))]),
+                axis_name="ctx",
+                split_axis=0,
+                concat_axis=0,
+            ),
+            axis=0,
+        ),
         lax.all_gather(v_head, "ctx", axis=0, tiled=True),
         q_pos,
     )

time: 651 us -> 683 us (1.049)
  waiting for transfers between devices: 416 us -> 437 us
  starting transfers between devices: 8.83 us -> 16.4 us
    all_to_all x0 -> x1, waiting for transfers between devices: none -> 131 us  [local(): lax.all_to_all(jnp.stack([k_head for _ in range(lax.axis_size('ctx'))]),...]
    all_gather x1 -> x0, waiting for transfers between devices: 77.6 us -> none  [local(): lax.all_gather(k_head, 'ctx', axis=0, tiled=True)]
    all_gather x1, waiting for transfers between devices: 43.9 us -> 0.02 us  [local(): lax.all_gather(v_head, 'ctx', axis=0, tiled=True)]
    unnamed x5 -> x4, waiting for transfers between devices: 137 us -> 149 us
    all_to_all x0 -> x1, starting transfers between devices: none -> 7.58 us  [local(): lax.all_to_all(jnp.stack([k_head for _ in range(lax.axis_size('ctx'))]),...]
  transfers between devices with their start and end apart: 5 -> 5, of which waited for: 4 -> 3; matrix products, arithmetic and copies ran while one was open for 6% -> 6% of each run, Pallas kernels for 0% -> 0%
where the time goes in v1:
time: 683 us; the launch traced here: 681 us
  waiting for transfers between devices  437 us (64%)
  blocking collectives  94 us (14%)
  matrix products  51.9 us (8%)
  local copies, waits for them, and re-layouts  44.5 us (7%)
  other arithmetic  23 us (3%)
  starting transfers between devices  16.4 us (2%)
  between operations  14.6 us (2%)
    psum x1, waiting for transfers between devices, local(): lax.psum(jnp.einsum('mxd,xdf->mxf', part_rows, w_gate_up, preferred_eleme...  157 us
    unnamed x4, waiting for transfers between devices  149 us
    all_to_all x1, waiting for transfers between devices, local(): lax.all_to_all(jnp.stack([k_head for _ in range(lax.axis_size('ctx'))]),...  131 us
    pmax x1, blocking collectives, local(): head_max = lax.pmax(head_peak, 'ctx')  37.2 us
    all_to_all x1, blocking collectives, local(): lax.all_to_all(lax.all_to_all(outgoing, 'ctx', split_axis=4, concat_axis=...  23.2 us
    dot_general x1, matrix products, attend_block(): jnp.einsum('rd,kd->rk', q_rows, k_block, preferred_element_type=jnp.float32)  19.1 us
    dot_general x1, matrix products, attend_block(): jnp.dot(weights.astype(jnp.bfloat16), v_block, preferred_element_type=jnp...  17.2 us
    all_to_all x1, blocking collectives, local(): lax.all_to_all(shaped, 'ctx', split_axis=1, concat_axis=4, tiled=True)  16.8 us
  transfers between devices with their start and end apart: 5, of which 3 were waited for; matrix products, arithmetic and copies ran while one was open for 6% of the time, Pallas kernels for 0%

profile of v1, /device:TPU:6, one launch (start us, length us, event | category | flops | bytes accessed | tf_op | source)
XLA Modules:
  0.0 681.4 jit_solution(3425378847347762580)
XLA Ops:
  10.4 4.8 stack.2
  15.2 7.6 %all-to-all-start = ((bf16[16,2048,128]{2,1,0:T(8,128)(2,1)}), bf16[16,2048,128]{2,1,0:T(8,128)(2,1)}, u32[]{:S(2)}, u32[]{:S(2)}) async-start(bf16[16,2048,128]{2,1,0:T(8,128)(2,1)} %stack.2), calls=%async_computation | async-start | bytes 16777216 | tf_op jit(solution)/shard_map/all_to_all | solution.py:63
  23.0 131.1 %all-to-all-done = bf16[16,2048,128]{2,1,0:T(8,128)(2,1)} async-done(((bf16[16,2048,128]{2,1,0:T(8,128)(2,1)}), bf16[16,2048,128]{2,1,0:T(8,128)(2,1)}, u32[]{:S(2)}, u32[]{:S(2)}) %all-to-all-start) | async-done | bytes 8388640 | tf_op jit(solution)/shard_map/all_to_all | solution.py:63
  154.1 19.1 %fusion.36 = (f32[256]{0:T(256)S(1)}, f32[256,32768]{0,1:T(8,128)}) fusion(bf16[32768,128]{1,0:T(8,128)(2,1)} %bitcast, bf16[256,128]{1,0:T(8,128)(2,1)S(1)} %bitcast.62, s32[256]{0:T(256)S(1)} %add.53), kind=kOutput, calls=%fused_computation.45 | convolution fusion | flops 2181037824 | bytes 42010624 | tf_op jit(solution)/shard_map/rd,kd->rk/dot_general | solution.py:21
  173.2 15.2 %fusion.2 = f32[256]{0:T(256)S(1)} fusion(f32[256,32768]{0,1:T(8,128)} %get-tuple-element.3, f32[256]{0:T(256)S(1)} %broadcast_maximum_fusion, s32[256]{0:T(256)S(1)} %add.53), kind=kLoop, calls=%fused_computation.5 | loop fusion | flops 33554176 | bytes 33557504 | tf_op jit(solution)/shard_map/reduce_sum | solution.py:28
  188.5 17.2 %fusion.19 = bf16[256,128]{1,0:T(8,128)(2,1)S(1)} fusion(bf16[32768,128]{1,0:T(8,128)(2,1)} %all-gather.2.cloned.1.call-done, f32[256,32768]{0,1:T(8,128)} %get-tuple-element.3, f32[256]{0:T(256)S(1)} %broadcast_maximum_fusion, s32[256]{0:T(256)S(1)} %add.53, f32[256]{0:T(256)S(1)} %fusion.2), kind=kOutput, calls=%fused_computation.18 | convolution fusion | flops 2181103616 | bytes 42011648 | tf_op jit(solution)/shard_map/dot_general | solution.py:29
  205.8 4.0 fusion.22
  211.9 148.9 %all-reduce.6.cloned.1.call-done = f32[64,4096]{1,0:T(8,128)} async-done(((f32[64,4096]{1,0:T(8,128)}), f32[64,4096]{1,0:T(8,128)}) %all-reduce.6.cloned.1.call-update) | async-done | bytes 1048592
  361.8 2.1 convolution_convert_fusion
  363.9 5.3 copy.33
  369.2 5.9 reshape.126
  375.1 16.8 %all_to_all.71 = bf16[16,2,8192]{2,1,0:T(2,128)(2,1)} all-to-all(bf16[16,2,8192]{2,1,0:T(2,128)(2,1)} %reshape.126), channel_id=1, replica_groups=mesh['ctx'=16,'exp'=16] {'ctx'}, dimensions={0} | all-to-all | bytes 1048576 | tf_op jit(solution)/shard_map/all_to_all | solution.py:112
  391.8 5.9 reshape.127
  397.7 4.1 copy.34
  401.9 23.2 %all_to_all.72 = bf16[1,16,2,32,256]{4,1,2,0,3:T(8,128)(2,1)S(1)} all-to-all(bf16[1,16,2,32,256]{4,1,2,0,3:T(8,128)(2,1)} %bitcast.57), channel_id=1, replica_groups=mesh['ctx'=16,'exp'=16] {'exp'}, dimensions={3} | all-to-all | bytes 1048576 | tf_op jit(solution)/shard_map/all_to_all | solution.py:111
  428.6 5.5 convert_bitcast_fusion
  434.1 157.1 %all-reduce.4.cloned.1.call-done = bf16[512,2,3072]{2,0,1:T(8,128)(2,1)} async-done(((bf16[512,2,3072]{2,0,1:T(8,128)(2,1)}), bf16[512,2,3072]{2,0,1:T(8,128)(2,1)}) %all-reduce.4.cloned.1.call-update) | async-done | bytes 6291472 | tf_op jit(solution)/shard_map/psum | solution.py:122
  591.2 4.5 convert_element_type.46
  595.8 2.7 fusion.12
  598.4 2.1 reshape.120
  601.8 16.8 %all_to_all.73 = bf16[16,16,2,2,256]{4,0,3,2,1:T(8,128)(2,1)S(1)} all-to-all(bf16[16,16,2,2,256]{4,0,3,2,1:T(8,128)(2,1)S(1)} %copy.37), channel_id=1, replica_groups=mesh['ctx'=16,'exp'=16] {'ctx'}, dimensions={1} | all-to-all | bytes 1048576 | tf_op jit(solution)/shard_map/all_to_all | solution.py:134
  621.7 8.5 %all-to-all-start.4 = ((bf16[16,1,2,2,4096]{4,3,2,1,0:T(2,128)(2,1)}), bf16[16,1,2,2,4096]{4,3,2,1,0:T(2,128)(2,1)}, u32[]{:S(2)}, u32[]{:S(2)}) async-start(bf16[16,1,2,2,4096]{4,3,2,1,0:T(2,128)(2,1)} %reshape.123), calls=%async_computation.4 | async-start | bytes 1048576 | tf_op jit(solution)/shard_map/all_to_all | solution.py:133
  630.4 37.2 %pmax.7 = f32[4]{0:T(128)} all-reduce(f32[4]{0:T(128)S(1)} %reduce_max.19), channel_id=1, replica_groups=mesh['ctx'=16,'exp'=16] {'ctx'}, use_global_device_ids=true, to_apply=%region_10.11 | all-reduce | flops 4 | bytes 32 | tf_op jit(solution)/shard_map/pmax | solution.py:81
  667.6 2.3 copy.40
  (54 shorter events, 19.0 us)
Async XLA Ops:
  7.2 421.4 %copy-start = (bf16[2,256,3072]{2,1,0:T(8,128)(2,1)S(1)}, bf16[2,256,3072]{2,1,0:T(8,128)(2,1)}, u32[]{:S(2)}) copy-start(bf16[2,256,3072]{2,1,0:T(8,128)(2,1)} %param.18) | copy-start | bytes 9437188
  7.2 181.3 %all-gather.2.cloned.1.call-start = ((), (), s32[]{:S(2)}) async-start(), calls=%async_computation.5 | async-start | bytes 8912896 | tf_op jit(solution)/shard_map/all_gather | solution.py:71
  15.2 7.7 %copy-start.2 = (bf16[64,512]{1,0:T(8,128)(2,1)S(1)}, bf16[64,512]{1,0:T(8,128)(2,1)}, u32[]{:S(2)}) copy-start(bf16[64,512]{1,0:T(8,128)(2,1)} %param.10) | copy-start | bytes 196612
  15.2 138.9 %all-to-all-start = ((bf16[16,2048,128]{2,1,0:T(8,128)(2,1)}), bf16[16,2048,128]{2,1,0:T(8,128)(2,1)}, u32[]{:S(2)}, u32[]{:S(2)}) async-start(bf16[16,2048,128]{2,1,0:T(8,128)(2,1)} %stack.2), calls=%async_computation | async-start | bytes 16777216 | tf_op jit(solution)/shard_map/all_to_all | solution.py:63
  22.8 337.9 %all-reduce.6.cloned.1.call-start = ((), (), s32[]{:S(2)}) async-start(), calls=%async_computation.7 | async-start | bytes 2097152
  188.4 21.6 %copy-start.4 = (s32[4,8]{1,0:T(4,128)S(1)}, s32[4,8]{1,0:T(4,128)}, u32[]{:S(2)}) copy-start(s32[4,8]{1,0:T(4,128)} %param.16) | copy-start | bytes 388
  188.4 22.1 %copy-start.7 = (u32[256]{0:T(256)S(1)}, u32[256]{0:T(256)}, u32[]{:S(2)}) copy-start(u32[256]{0:T(256)} %constant.65) | copy-start | bytes 3076
  188.4 172.3 %copy-start.1 = (bf16[4,4096]{1,0:T(4,128)(2,1)S(1)}, bf16[4,4096]{1,0:T(4,128)(2,1)}, u32[]{:S(2)}) copy-start(bf16[4,4096]{1,0:T(4,128)(2,1)} %param.14) | copy-start | bytes 98308
  188.5 173.4 %copy-start.3 = (f32[4096]{0:T(1024)S(1)}, f32[4096]{0:T(1024)}, u32[]{:S(2)}) copy-start(f32[4096]{0:T(1024)} %param.15) | copy-start | bytes 49156
  209.8 381.4 %all-reduce.4.cloned.1.call-start = ((), (), s32[]{:S(2)}) async-start(), calls=%async_computation.6 | async-start | bytes 12582912 | tf_op jit(solution)/shard_map/psum | solution.py:122
  591.2 4.6 copy-start.6
  598.4 73.5 %copy-start.5 = (f32[4,8]{1,0:T(4,128)S(1)}, f32[4,8]{1,0:T(4,128)}, u32[]{:S(2)}) copy-start(f32[4,8]{1,0:T(4,128)} %param.17) | copy-start | bytes 388
  621.7 45.9 %all-to-all-start.4 = ((bf16[16,1,2,2,4096]{4,3,2,1,0:T(2,128)(2,1)}), bf16[16,1,2,2,4096]{4,3,2,1,0:T(2,128)(2,1)}, u32[]{:S(2)}, u32[]{:S(2)}) async-start(bf16[16,1,2,2,4096]{4,3,2,1,0:T(2,128)(2,1)} %reshape.123), calls=%async_computation.4 | async-start | bytes 1048576 | tf_op jit(solution)/shard_map/all_to_all | solution.py:133
Sparse Core Ops, SparseCore 0:
  10.7 165.5 all-gather.1
  209.9 150.7 all-reduce.5
  434.2 156.9 all-reduce.3
